TPU v7x, 32 devices: a whole 2x2x4 slice. The times are simulated.
32 devices in a mesh: tm: 4 (over x, core), space: 8 (over z, y).
Axes of the slice: x: 2, y: 2, z: 4, core: 2. Of those that a mesh axis runs over, the one named last changes fastest.
Arguments:
- cotangent: bfloat16 [16, 64, 8192], P('tm', 'space'), may hold values from -6 to 6
- saved_mix: bfloat16 [16, 64, 8192], P('tm', 'space'), may hold values from -6 to 6
- saved_pre: bfloat16 [16, 64, 8192], P('tm', 'space'), may hold values from -8 to 8
- kernel_one: bfloat16 [4, 3, 3, 64, 64], replicated, may hold values from -0.25 to 0.25
- kernel_two: bfloat16 [4, 3, 3, 64, 64], replicated, may hold values from -0.25 to 0.25
- ref_pairs: int32 [16, 2], replicated, may hold values from 0 to 15, as said below
- frame_level: int32 [16], replicated, may hold values from 0 to 4, as said below
Outputs:
- input_grad: float32 [16, 64, 8192], P('tm', 'space')
- weight_grad_one: float32 [4, 3, 3, 64, 64], replicated
- weight_grad_two: float32 [4, 3, 3, 64, 64], replicated
Inputs may be any that keep to these rules, and one draw needn't show every extreme that they name: Frame c was predicted from frames ref_pairs[c, 0] and ref_pairs[c, 1]; for a frame of level k >= 1 both have a level below k (at level 1 both name the level-0 frame); the level-0 frame names itself twice. `frame_level`: one frame has level 0 and 2**(k-1) frames have level k for k from 1 to 4; frames are stored in an order drawn from the seed.
All inputs are finite; a program needn't handle non-finite values.
Results may differ from a plain program's by a relative error of at most 0.006.
Values may be sent and summed in bfloat16 or wider, within the bound.
A program may use at most 64 MiB of HBM per device.

v0:
```python
import math
import jax
import jax.numpy as jnp
from jax import lax
from jax.sharding import PartitionSpec as P


def padded_2(cells, sides, width):
    for axis, dim in sides:
        count = lax.axis_size(axis)
        ends = count - 1
        head = lax.slice_in_dim(cells, 0, width, axis=dim)
        tail = lax.slice_in_dim(cells, cells.shape[dim] - width, cells.shape[dim], axis=dim)
        cells = jnp.concatenate(
            [
                lax.ppermute(tail, axis, [(i, (i + 1) % count) for i in range(ends)]),
                cells,
                lax.ppermute(head, axis, [((i + 1) % count, i) for i in range(ends)]),
            ],
            axis=dim,
        )
    return cells


def flipped(kernel):
    return jnp.transpose(kernel[::-1, ::-1], (0, 1, 3, 2))


def pair_kernel(kernel):
    blank = jnp.zeros_like(kernel[:, 0])
    row_blocks = []
    for in_part in range(4):
        col_blocks = []
        for out_half in range(2):
            col_tap = in_part - out_half
            col_blocks.append(kernel[:, col_tap] if 0 <= col_tap <= 2 else blank)
        row_blocks.append(jnp.concatenate(col_blocks, axis=-1))
    return jnp.concatenate(row_blocks, axis=1)


def pair_view(field, channels):
    col_count = field.shape[2] // channels
    grid = field.reshape(field.shape[0], field.shape[1], col_count, channels)
    grid = jnp.pad(grid, ((0, 0), (0, 0), (1, 1), (0, 0)))
    grid = grid.reshape(field.shape[0], field.shape[1], (col_count + 2) // 2, 2 * channels)
    return jnp.concatenate((grid[:, :, :-1], grid[:, :, 1:]), axis=-1)


def conv_taps(field, paired):
    channels = paired.shape[2] // 2
    windows = pair_view(field, channels)
    row_count = field.shape[1] - 2
    result = jnp.einsum(
        "nrjk,kc->nrjc", windows[:, 0:row_count], paired[0], preferred_element_type=jnp.float32
    )
    for row_tap in range(1, 3):
        result = result + jnp.einsum(
            "nrjk,kc->nrjc",
            windows[:, row_tap : row_tap + row_count],
            paired[row_tap],
            preferred_element_type=jnp.float32,
        )
    return result.reshape(field.shape[0], row_count, -1)


def correlate(field, cot, channels):
    windows = pair_view(field, channels)
    row_count = cot.shape[1]
    cot_pairs = cot.reshape(cot.shape[0], row_count, -1, 2 * channels)
    taps = []
    for row_tap in range(3):
        blocks = jnp.einsum(
            "nrjk,nrjc->nkc",
            windows[:, row_tap : row_tap + row_count],
            cot_pairs,
            preferred_element_type=jnp.float32,
        )
        row_taps = []
        for col_tap in range(3):
            first_part = blocks[:, col_tap * channels : (col_tap + 1) * channels, 0:channels]
            second_part = blocks[
                :, (col_tap + 1) * channels : (col_tap + 2) * channels, channels : 2 * channels
            ]
            row_taps.append(first_part + second_part)
        taps.append(jnp.stack(row_taps, axis=1))
    return jnp.stack(taps, axis=1)


def backprop(slot_cot, slot_slope, kernel_inner, kernel_outer):
    padded = padded_2(slot_cot, (("space", 1),), 1)
    slot_grad = (conv_taps(padded, kernel_inner) * slot_slope).astype(jnp.bfloat16)
    grad_padded = padded_2(slot_grad, (("space", 1),), 1)
    to_refs = conv_taps(grad_padded, kernel_outer).astype(jnp.bfloat16)
    return (slot_grad, to_refs)


def body_time(cotangent, saved_mix, saved_pre, kernel_one, kernel_two, ref_pairs, frame_level):
    frames_dev = cotangent.shape[0]
    row_count = cotangent.shape[1]
    channels = kernel_one.shape[-1]
    levels_all = kernel_one.shape[0]
    col_count = cotangent.shape[2] // channels
    first_frame = lax.axis_index("tm") * frames_dev
    local_ids = first_frame + jnp.arange(frames_dev, dtype=jnp.int32)
    local_level = lax.dynamic_slice_in_dim(frame_level, first_frame, frames_dev, 0)
    frame_count = ref_pairs.shape[0]
    all_frames = jnp.arange(frame_count, dtype=jnp.int32)
    preact = saved_pre.astype(jnp.float32)
    sigmoid_pre = jax.nn.sigmoid(preact)
    act_slope = sigmoid_pre * (1.0 + preact * (1.0 - sigmoid_pre))
    act_out = (preact * sigmoid_pre).astype(jnp.bfloat16)
    saved_rims = padded_2(jnp.stack((saved_mix, act_out)), (("space", 2),), 1)
    cot_total = cotangent.astype(jnp.float32)
    kept_grad = jnp.zeros_like(cotangent)
    for level_now in range(levels_all, 0, -1):
        active = local_level == level_now
        slot_count = min(frames_dev, 2 ** (level_now - 1))
        ranks = jnp.cumsum(active.astype(jnp.int32)) - 1
        picker = jnp.logical_and(
            ranks[None, :] == jnp.arange(slot_count, dtype=jnp.int32)[:, None], active[None, :]
        )
        picker_wide = picker.astype(jnp.float32)
        slot_cot = jnp.einsum(
            "sf,fx->sx",
            picker.astype(jnp.bfloat16),
            cot_total.astype(jnp.bfloat16).reshape(frames_dev, -1),
            preferred_element_type=jnp.float32,
        )
        slot_cot = slot_cot.astype(jnp.bfloat16).reshape(slot_count, row_count, -1)
        slot_slope = jnp.einsum(
            "sf,fx->sx",
            picker_wide,
            act_slope.reshape(frames_dev, -1),
            precision=lax.Precision.HIGHEST,
        ).reshape(slot_count, row_count, -1)
        slot_ids = jnp.sum(picker.astype(jnp.int32) * local_ids[None, :], axis=1)
        slot_ok = jnp.sum(picker.astype(jnp.int32), axis=1)
        kernel_inner = pair_kernel(flipped(kernel_two[level_now - 1]))
        kernel_outer = pair_kernel(flipped(kernel_one[level_now - 1]))
        slot_grad, to_refs = backprop(slot_cot, slot_slope, kernel_inner, kernel_outer)
        frame_grad = jnp.einsum(
            "sf,sx->fx",
            picker.astype(jnp.bfloat16),
            slot_grad.reshape(slot_grad.shape[0], -1),
            preferred_element_type=jnp.float32,
        )
        frame_grad = frame_grad.astype(jnp.bfloat16).reshape(kept_grad.shape)
        kept_grad = jnp.where(active[:, None, None], frame_grad, kept_grad)
        moved = lax.all_gather(to_refs, "tm", axis=0, tiled=True)
        sender_ids = lax.all_gather(slot_ids, "tm", axis=0, tiled=True)
        sender_ok = lax.all_gather(slot_ok, "tm", axis=0, tiled=True)
        matches = (sender_ids[:, None] == all_frames[None, :]).astype(jnp.int32)
        first_ref = jnp.sum(matches * ref_pairs[None, :, 0], axis=1)
        second_ref = jnp.sum(matches * ref_pairs[None, :, 1], axis=1)
        hits = (first_ref[:, None] == local_ids[None, :]).astype(jnp.float32) + (
            second_ref[:, None] == local_ids[None, :]
        ).astype(jnp.float32)
        weights = 0.5 * sender_ok[:, None].astype(jnp.float32) * hits
        added = jnp.einsum(
            "kf,kx->fx",
            weights.astype(jnp.bfloat16),
            moved.reshape(moved.shape[0], -1),
            preferred_element_type=jnp.float32,
        )
        cot_total = cot_total + added.reshape(cot_total.shape)
    final_cot = cot_total.astype(jnp.bfloat16)
    per_one = correlate(saved_rims[0], kept_grad, channels)
    per_two = correlate(saved_rims[1], final_cot, channels)
    level_hot = (
        local_level[:, None] == jnp.arange(1, levels_all + 1, dtype=jnp.int32)[None, :]
    ).astype(jnp.float32)
    scale = 1.0 / math.sqrt(row_count * lax.axis_size("space") * col_count)
    sum_one = scale * jnp.sum(level_hot[:, :, None, None, None, None] * per_one[:, None], axis=0)
    sum_two = scale * jnp.sum(level_hot[:, :, None, None, None, None] * per_two[:, None], axis=0)
    weight_one, weight_two = lax.psum((sum_one, sum_two), ("tm", "space"))
    return (cot_total, weight_one, weight_two)


def on_device(cotangent, saved_mix, saved_pre, kernel_one, kernel_two, ref_pairs, frame_level):
    return body_time(
        cotangent, saved_mix, saved_pre, kernel_one, kernel_two, ref_pairs, frame_level
    )


def solution(mesh):
    placed = (
        P("tm", "space", None),
        P("tm", "space", None),
        P("tm", "space", None),
        P(),
        P(),
        P(),
        P(),
    )
    return jax.shard_map(
        on_device,
        mesh=mesh,
        in_specs=placed,
        out_specs=(P("tm", "space", None), P(), P()),
        check_vma=False,
    )
```

profile of v0, /device:TPU:0, one launch (start us, length us, event | category | flops | bytes accessed | tf_op | source)
XLA Modules:
  0.0 384.8 jit_solution(5619695112859020218)
XLA Ops:
  13.1 4.9 %collective-permute-start = (bf16[4,1,8192]{2,0,1:T(4,128)(2,1)S(1)}, bf16[4,1,8192]{2,0,1:T(4,128)(2,1)S(1)}, u32[]{:S(2)}, u32[]{:S(2)}) collective-permute-start(bf16[4,1,8192]{2,0,1:T(4,128)(2,1)S(1)} %get-tuple-element.102), channel_id=1, source_target_pairs={{0,1},{1,2},{2,3},{3,4},{4,5},{5,6},{6,7},{8,9},{9,10},{10,11},{11... | collective-permute-start | bytes 196616 | tf_op jit(solution)/shard_map/ppermute | solution.py:16
  34.6 4.6 %collective-permute-start.2 = (bf16[4,1,8192]{2,0,1:T(4,128)(2,1)S(1)}, bf16[4,1,8192]{2,0,1:T(4,128)(2,1)S(1)}, u32[]{:S(2)}, u32[]{:S(2)}) collective-permute-start(bf16[4,1,8192]{2,0,1:T(4,128)(2,1)S(1)} %get-tuple-element.100), channel_id=1, source_target_pairs={{0,1},{1,2},{2,3},{3,4},{4,5},{5,6},{6,7},{8,9},{9,10},{10,11},{11... | collective-permute-start | bytes 196616 | tf_op jit(solution)/shard_map/ppermute | solution.py:16
  41.0 4.7 %collective-permute-done.3 = bf16[4,1,8192]{2,0,1:T(4,128)(2,1)S(1)} collective-permute-done((bf16[4,1,8192]{2,0,1:T(4,128)(2,1)S(1)}, bf16[4,1,8192]{2,0,1:T(4,128)(2,1)S(1)}, u32[]{:S(2)}, u32[]{:S(2)}) %collective-permute-start.3) | collective-permute-done | bytes 65568 | tf_op jit(solution)/shard_map/ppermute | solution.py:18
  55.1 5.7 %collective-permute-start.16 = (bf16[2,4,1,8192]{3,2,1,0:T(2,128)(2,1)}, bf16[2,4,1,8192]{3,2,1,0:T(2,128)(2,1)}, u32[]{:S(2)}, u32[]{:S(2)}) collective-permute-start(bf16[2,4,1,8192]{3,2,1,0:T(2,128)(2,1)} %get-tuple-element.54), channel_id=1, source_target_pairs={{0,1},{1,2},{2,3},{3,4},{4,5},{5,6},{6,7},{8,9},{9,10},{10,11},{11... | collective-permute-start | bytes 393224 | tf_op jit(solution)/shard_map/ppermute | solution.py:16
  69.0 5.7 %all-reduce.34 = (s32[16]{0:T(128)S(1)}, s32[16]{0:T(128)S(1)}, s32[16]{0:T(128)S(1)}, s32[16]{0:T(128)}, s32[8]{0:T(128)S(1)}, /*index=5*/s32[8]{0:T(128)}, s32[4]{0:T(128)S(1)}, s32[4]{0:T(128)}) all-reduce(s32[16]{0:T(128)S(1)} %dynamic-update-slice.3, s32[16]{0:T(128)S(1)} %dynamic-update-slice.1, ...), channel_id=1, replica_groups=mesh['tm'=4,'space'=8] {'tm'}, use_global_device_ids=true, to_apply=%add.29 | all-reduce | flops 88 | bytes 704
  78.1 5.5 %fusion.214 = (bf16[4,8,8192]{2,0,1:T(4,128)(2,1)S(1)}, f32[4,8,8192]{2,0,1:T(4,128)}) fusion(s32[16]{0:T(128)S(1)} %get-tuple-element.31, s32[16]{0:T(128)S(1)} %get-tuple-element.30, f32[16]{0:T(128)S(1)} %convert_multiply_fusion.5, s32[4]{0:T(128)S(1)} %get-tuple-element.160, bf16[4,8,8192]{2,1,0:T(8,128)(2,1)S(1)} %copy-done.31, ...), kind=kOutput, calls=%fused_computation.415 | convolution fusion | flops 9175488 | bytes 4194512 | tf_op jit(solution)/shard_map/kf,kx->fx/dot_general | solution.py:159
  84.2 3.4 collective-permute-start.4
  101.7 4.3 %collective-permute-start.6 = (bf16[4,1,8192]{2,0,1:T(4,128)(2,1)S(1)}, bf16[4,1,8192]{2,0,1:T(4,128)(2,1)S(1)}, u32[]{:S(2)}, u32[]{:S(2)}) collective-permute-start(bf16[4,1,8192]{2,0,1:T(4,128)(2,1)S(1)} %get-tuple-element.96), channel_id=1, source_target_pairs={{0,1},{1,2},{2,3},{3,4},{4,5},{5,6},{6,7},{8,9},{9,10},{10,11},{11... | collective-permute-start | bytes 196616 | tf_op jit(solution)/shard_map/ppermute | solution.py:16
  107.9 4.3 %collective-permute-done.7 = bf16[4,1,8192]{2,0,1:T(4,128)(2,1)S(1)} collective-permute-done((bf16[4,1,8192]{2,0,1:T(4,128)(2,1)S(1)}, bf16[4,1,8192]{2,0,1:T(4,128)(2,1)S(1)}, u32[]{:S(2)}, u32[]{:S(2)}) %collective-permute-start.7) | collective-permute-done | bytes 65568 | tf_op jit(solution)/shard_map/ppermute | solution.py:18
  124.9 2.4 fusion.143
  127.2 15.2 %all-gather.6.cloned.1.call-done = bf16[16,8,8192]{2,1,0:T(8,128)(2,1)} async-done(((bf16[4,8,8192]{2,1,0:T(8,128)(2,1)}), bf16[16,8,8192]{2,1,0:T(8,128)(2,1)}) %all-gather.6.cloned.1.call-update) | async-done | bytes 2097168 | tf_op jit(solution)/shard_map/all_gather | solution.py:149
  142.4 5.2 %fusion.215 = (bf16[4,8,8192]{2,0,1:T(4,128)(2,1)S(1)}, f32[4,8,8192]{2,0,1:T(4,128)}) fusion(f32[4,8,8192]{2,0,1:T(4,128)S(1)} %copy-done.14, s32[16]{0:T(128)S(1)} %get-tuple-element.32, s32[16]{0:T(128)S(1)} %get-tuple-element.29, f32[16]{0:T(128)S(1)} %convert_multiply_fusion.4, s32[4]{0:T(128)S(1)} %get-tuple-element.160, ...), kind=kOutput, calls=%fused_computation.416 | convolution fusion | flops 8913344 | bytes 4718800 | tf_op jit(solution)/shard_map/kf,kx->fx/dot_general | solution.py:159
  148.1 3.4 collective-permute-start.8
  154.5 2.7 collective-permute-done.9
  161.3 4.3 %collective-permute-start.10 = (bf16[2,1,8192]{2,0,1:T(2,128)(2,1)S(1)}, bf16[2,1,8192]{2,0,1:T(2,128)(2,1)S(1)}, u32[]{:S(2)}, u32[]{:S(2)}) collective-permute-start(bf16[2,1,8192]{2,0,1:T(2,128)(2,1)S(1)} %get-tuple-element.108), channel_id=1, source_target_pairs={{0,1},{1,2},{2,3},{3,4},{4,5},{5,6},{6,7},{8,9},{9,10},{10,11},{11... | collective-permute-start | bytes 98312 | tf_op jit(solution)/shard_map/ppermute | solution.py:16
  189.4 3.3 all-gather.8.cloned.1.call-done
  192.7 2.7 fusion.216
  196.0 3.4 collective-permute-start.12
  201.9 3.3 collective-permute-done.13
  211.1 4.3 %collective-permute-start.14 = (bf16[1,1,8192]{2,1,0:T(2,128)(2,1)S(1)}, bf16[1,1,8192]{2,1,0:T(2,128)(2,1)S(1)}, u32[]{:S(2)}, u32[]{:S(2)}) collective-permute-start(bf16[1,1,8192]{2,1,0:T(2,128)(2,1)S(1)} %get-tuple-element.140), channel_id=1, source_target_pairs={{0,1},{1,2},{2,3},{3,4},{4,5},{5,6},{6,7},{8,9},{9,10},{10,11},{11... | collective-permute-start | bytes 49160 | tf_op jit(solution)/shard_map/ppermute | solution.py:16
  218.5 2.7 collective-permute-done.15
  222.6 6.5 %all_gather.47 = bf16[4,8,8192]{2,1,0:T(8,128)(2,1)S(1)} all-gather(bf16[1,8,8192]{2,1,0:T(8,128)(2,1)S(1)} %convert_element_type.244), channel_id=1, replica_groups=mesh['tm'=4,'space'=8] {'tm'}, dimensions={0}, use_global_device_ids=true | all-gather | bytes 655360 | tf_op jit(solution)/shard_map/all_gather | solution.py:149
  240.2 134.1 %all-reduce.38.cloned.1.call-done = (f32[4,3,3,64,64]{4,3,2,1,0:T(8,128)}, f32[4,3,3,64,64]{4,3,2,1,0:T(8,128)}) async-done(((f32[4,3,3,64,64]{4,3,2,1,0:T(8,128)}, f32[4,3,3,64,64]{4,3,2,1,0:T(8,128)}), (f32[4,3,3,64,64]{4,3,2,1,0:T(8,128)}, f32[4,3,3,64,64]{4,3,2,1,0:T(8,128)})) %all-reduce.38.cloned.1.call-update) | async-done | bytes 1179664 | tf_op jit(solution)/shard_map/psum | solution.py:175
  374.3 2.5 copy.332
  (377 shorter events, 128.6 us)
Async XLA Ops:
  7.2 70.9 %all-gather.4.cloned.1.call-start = ((), (), s32[]{:S(2)}) async-start(), calls=%async_computation | async-start | bytes 2621440 | tf_op jit(solution)/shard_map/all_gather | solution.py:149
  9.3 56.3 %copy-start.39 = (pred[4]{0:T(512)(128)(4,1)}, pred[4]{0:T(512)(128)(4,1)S(1)}, u32[]{:S(2)}) copy-start(pred[4]{0:T(512)(128)(4,1)S(1)} %get-tuple-element.149) | copy-start | bytes 16
  13.1 12.7 %collective-permute-start = (bf16[4,1,8192]{2,0,1:T(4,128)(2,1)S(1)}, bf16[4,1,8192]{2,0,1:T(4,128)(2,1)S(1)}, u32[]{:S(2)}, u32[]{:S(2)}) collective-permute-start(bf16[4,1,8192]{2,0,1:T(4,128)(2,1)S(1)} %get-tuple-element.102), channel_id=1, source_target_pairs={{0,1},{1,2},{2,3},{3,4},{4,5},{5,6},{6,7},{8,9},{9,10},{10,11},{11... | collective-permute-start | bytes 196616 | tf_op jit(solution)/shard_map/ppermute | solution.py:16
  18.0 8.6 %collective-permute-start.1 = (bf16[4,1,8192]{2,0,1:T(4,128)(2,1)S(1)}, bf16[4,1,8192]{2,0,1:T(4,128)(2,1)S(1)}, u32[]{:S(2)}, u32[]{:S(2)}) collective-permute-start(bf16[4,1,8192]{2,0,1:T(4,128)(2,1)S(1)} %get-tuple-element.103), channel_id=1, source_target_pairs={{1,0},{2,1},{3,2},{4,3},{5,4},{6,5},{7,6},{9,8},{10,9},{11,10},{12... | collective-permute-start | bytes 196616 | tf_op jit(solution)/shard_map/ppermute | solution.py:18
  34.6 6.4 %collective-permute-start.2 = (bf16[4,1,8192]{2,0,1:T(4,128)(2,1)S(1)}, bf16[4,1,8192]{2,0,1:T(4,128)(2,1)S(1)}, u32[]{:S(2)}, u32[]{:S(2)}) collective-permute-start(bf16[4,1,8192]{2,0,1:T(4,128)(2,1)S(1)} %get-tuple-element.100), channel_id=1, source_target_pairs={{0,1},{1,2},{2,3},{3,4},{4,5},{5,6},{6,7},{8,9},{9,10},{10,11},{11... | collective-permute-start | bytes 196616 | tf_op jit(solution)/shard_map/ppermute | solution.py:16
  39.2 6.6 %collective-permute-start.3 = (bf16[4,1,8192]{2,0,1:T(4,128)(2,1)S(1)}, bf16[4,1,8192]{2,0,1:T(4,128)(2,1)S(1)}, u32[]{:S(2)}, u32[]{:S(2)}) collective-permute-start(bf16[4,1,8192]{2,0,1:T(4,128)(2,1)S(1)} %get-tuple-element.101), channel_id=1, source_target_pairs={{1,0},{2,1},{3,2},{4,3},{5,4},{6,5},{7,6},{9,8},{10,9},{11,10},{12... | collective-permute-start | bytes 196616 | tf_op jit(solution)/shard_map/ppermute | solution.py:18
  53.6 88.8 %all-gather.6.cloned.1.call-start = ((), (), s32[]{:S(2)}) async-start(), calls=%async_computation.1 | async-start | bytes 2621440 | tf_op jit(solution)/shard_map/all_gather | solution.py:149
  55.1 23.0 %copy-start.31 = (bf16[4,8,8192]{2,1,0:T(8,128)(2,1)S(1)}, bf16[4,8,8192]{2,1,0:T(8,128)(2,1)}, u32[]{:S(2)}) copy-start(bf16[4,8,8192]{2,1,0:T(8,128)(2,1)} %param.7) | copy-start | bytes 1572868
  55.1 112.0 %collective-permute-start.16 = (bf16[2,4,1,8192]{3,2,1,0:T(2,128)(2,1)}, bf16[2,4,1,8192]{3,2,1,0:T(2,128)(2,1)}, u32[]{:S(2)}, u32[]{:S(2)}) collective-permute-start(bf16[2,4,1,8192]{3,2,1,0:T(2,128)(2,1)} %get-tuple-element.54), channel_id=1, source_target_pairs={{0,1},{1,2},{2,3},{3,4},{4,5},{5,6},{6,7},{8,9},{9,10},{10,11},{11... | collective-permute-start | bytes 393224 | tf_op jit(solution)/shard_map/ppermute | solution.py:16
  60.8 106.3 %collective-permute-start.17 = (bf16[2,4,1,8192]{3,2,1,0:T(2,128)(2,1)}, bf16[2,4,1,8192]{3,2,1,0:T(2,128)(2,1)}, u32[]{:S(2)}, u32[]{:S(2)}) collective-permute-start(bf16[2,4,1,8192]{3,2,1,0:T(2,128)(2,1)} %get-tuple-element.55), channel_id=1, source_target_pairs={{1,0},{2,1},{3,2},{4,3},{5,4},{6,5},{7,6},{9,8},{10,9},{11,10},{12... | collective-permute-start | bytes 393224 | tf_op jit(solution)/shard_map/ppermute | solution.py:18
  84.2 6.7 %collective-permute-start.4 = (bf16[4,1,8192]{2,0,1:T(4,128)(2,1)S(1)}, bf16[4,1,8192]{2,0,1:T(4,128)(2,1)S(1)}, u32[]{:S(2)}, u32[]{:S(2)}) collective-permute-start(bf16[4,1,8192]{2,0,1:T(4,128)(2,1)S(1)} %get-tuple-element.98), channel_id=1, source_target_pairs={{0,1},{1,2},{2,3},{3,4},{4,5},{5,6},{6,7},{8,9},{9,10},{10,11},{11... | collective-permute-start | bytes 196616 | tf_op jit(solution)/shard_map/ppermute | solution.py:16
  87.6 6.2 %collective-permute-start.5 = (bf16[4,1,8192]{2,0,1:T(4,128)(2,1)S(1)}, bf16[4,1,8192]{2,0,1:T(4,128)(2,1)S(1)}, u32[]{:S(2)}, u32[]{:S(2)}) collective-permute-start(bf16[4,1,8192]{2,0,1:T(4,128)(2,1)S(1)} %get-tuple-element.99), channel_id=1, source_target_pairs={{1,0},{2,1},{3,2},{4,3},{5,4},{6,5},{7,6},{9,8},{10,9},{11,10},{12... | collective-permute-start | bytes 196616 | tf_op jit(solution)/shard_map/ppermute | solution.py:18
  101.7 6.2 %collective-permute-start.6 = (bf16[4,1,8192]{2,0,1:T(4,128)(2,1)S(1)}, bf16[4,1,8192]{2,0,1:T(4,128)(2,1)S(1)}, u32[]{:S(2)}, u32[]{:S(2)}) collective-permute-start(bf16[4,1,8192]{2,0,1:T(4,128)(2,1)S(1)} %get-tuple-element.96), channel_id=1, source_target_pairs={{0,1},{1,2},{2,3},{3,4},{4,5},{5,6},{6,7},{8,9},{9,10},{10,11},{11... | collective-permute-start | bytes 196616 | tf_op jit(solution)/shard_map/ppermute | solution.py:16
  106.0 6.2 %collective-permute-start.7 = (bf16[4,1,8192]{2,0,1:T(4,128)(2,1)S(1)}, bf16[4,1,8192]{2,0,1:T(4,128)(2,1)S(1)}, u32[]{:S(2)}, u32[]{:S(2)}) collective-permute-start(bf16[4,1,8192]{2,0,1:T(4,128)(2,1)S(1)} %get-tuple-element.97), channel_id=1, source_target_pairs={{1,0},{2,1},{3,2},{4,3},{5,4},{6,5},{7,6},{9,8},{10,9},{11,10},{12... | collective-permute-start | bytes 196616 | tf_op jit(solution)/shard_map/ppermute | solution.py:18
  120.5 72.2 %all-gather.8.cloned.1.call-start = ((), (), s32[]{:S(2)}) async-start(), calls=%async_computation.2 | async-start | bytes 1310720 | tf_op jit(solution)/shard_map/all_gather | solution.py:149
  148.1 6.3 %collective-permute-start.8 = (bf16[2,1,8192]{2,0,1:T(2,128)(2,1)S(1)}, bf16[2,1,8192]{2,0,1:T(2,128)(2,1)S(1)}, u32[]{:S(2)}, u32[]{:S(2)}) collective-permute-start(bf16[2,1,8192]{2,0,1:T(2,128)(2,1)S(1)} %get-tuple-element.110), channel_id=1, source_target_pairs={{0,1},{1,2},{2,3},{3,4},{4,5},{5,6},{6,7},{8,9},{9,10},{10,11},{11... | collective-permute-start | bytes 98312 | tf_op jit(solution)/shard_map/ppermute | solution.py:16
  151.5 5.8 %collective-permute-start.9 = (bf16[2,1,8192]{2,0,1:T(2,128)(2,1)S(1)}, bf16[2,1,8192]{2,0,1:T(2,128)(2,1)S(1)}, u32[]{:S(2)}, u32[]{:S(2)}) collective-permute-start(bf16[2,1,8192]{2,0,1:T(2,128)(2,1)S(1)} %get-tuple-element.111), channel_id=1, source_target_pairs={{1,0},{2,1},{3,2},{4,3},{5,4},{6,5},{7,6},{9,8},{10,9},{11,10},{12... | collective-permute-start | bytes 98312 | tf_op jit(solution)/shard_map/ppermute | solution.py:18
  161.3 7.8 %collective-permute-start.10 = (bf16[2,1,8192]{2,0,1:T(2,128)(2,1)S(1)}, bf16[2,1,8192]{2,0,1:T(2,128)(2,1)S(1)}, u32[]{:S(2)}, u32[]{:S(2)}) collective-permute-start(bf16[2,1,8192]{2,0,1:T(2,128)(2,1)S(1)} %get-tuple-element.108), channel_id=1, source_target_pairs={{0,1},{1,2},{2,3},{3,4},{4,5},{5,6},{6,7},{8,9},{9,10},{10,11},{11... | collective-permute-start | bytes 98312 | tf_op jit(solution)/shard_map/ppermute | solution.py:16
  165.6 5.8 %collective-permute-start.11 = (bf16[2,1,8192]{2,0,1:T(2,128)(2,1)S(1)}, bf16[2,1,8192]{2,0,1:T(2,128)(2,1)S(1)}, u32[]{:S(2)}, u32[]{:S(2)}) collective-permute-start(bf16[2,1,8192]{2,0,1:T(2,128)(2,1)S(1)} %get-tuple-element.109), channel_id=1, source_target_pairs={{1,0},{2,1},{3,2},{4,3},{5,4},{6,5},{7,6},{9,8},{10,9},{11,10},{12... | collective-permute-start | bytes 98312 | tf_op jit(solution)/shard_map/ppermute | solution.py:18
  176.8 197.5 %all-reduce.38.cloned.1.call-start = ((), (), s32[]{:S(2)}) async-start(), calls=%async_computation.3 | async-start | bytes 4718592 | tf_op jit(solution)/shard_map/psum | solution.py:175
  196.0 5.7 %collective-permute-start.12 = (bf16[1,1,8192]{2,1,0:T(2,128)(2,1)S(1)}, bf16[1,1,8192]{2,1,0:T(2,128)(2,1)S(1)}, u32[]{:S(2)}, u32[]{:S(2)}) collective-permute-start(bf16[1,1,8192]{2,1,0:T(2,128)(2,1)S(1)} %get-tuple-element.142), channel_id=1, source_target_pairs={{0,1},{1,2},{2,3},{3,4},{4,5},{5,6},{6,7},{8,9},{9,10},{10,11},{11... | collective-permute-start | bytes 49160 | tf_op jit(solution)/shard_map/ppermute | solution.py:16
  199.4 5.8 %collective-permute-start.13 = (bf16[1,1,8192]{2,1,0:T(2,128)(2,1)S(1)}, bf16[1,1,8192]{2,1,0:T(2,128)(2,1)S(1)}, u32[]{:S(2)}, u32[]{:S(2)}) collective-permute-start(bf16[1,1,8192]{2,1,0:T(2,128)(2,1)S(1)} %get-tuple-element.143), channel_id=1, source_target_pairs={{1,0},{2,1},{3,2},{4,3},{5,4},{6,5},{7,6},{9,8},{10,9},{11,10},{12... | collective-permute-start | bytes 49160 | tf_op jit(solution)/shard_map/ppermute | solution.py:18
  211.1 7.2 %collective-permute-start.14 = (bf16[1,1,8192]{2,1,0:T(2,128)(2,1)S(1)}, bf16[1,1,8192]{2,1,0:T(2,128)(2,1)S(1)}, u32[]{:S(2)}, u32[]{:S(2)}) collective-permute-start(bf16[1,1,8192]{2,1,0:T(2,128)(2,1)S(1)} %get-tuple-element.140), channel_id=1, source_target_pairs={{0,1},{1,2},{2,3},{3,4},{4,5},{5,6},{6,7},{8,9},{9,10},{10,11},{11... | collective-permute-start | bytes 49160 | tf_op jit(solution)/shard_map/ppermute | solution.py:16
  215.4 5.8 %collective-permute-start.15 = (bf16[1,1,8192]{2,1,0:T(2,128)(2,1)S(1)}, bf16[1,1,8192]{2,1,0:T(2,128)(2,1)S(1)}, u32[]{:S(2)}, u32[]{:S(2)}) collective-permute-start(bf16[1,1,8192]{2,1,0:T(2,128)(2,1)S(1)} %get-tuple-element.141), channel_id=1, source_target_pairs={{1,0},{2,1},{3,2},{4,3},{5,4},{6,5},{7,6},{9,8},{10,9},{11,10},{12... | collective-permute-start | bytes 49160 | tf_op jit(solution)/shard_map/ppermute | solution.py:18
  (60 other events, 303.9 us)
Sparse Core Ops, SparseCore 0:
  53.7 24.2 all-gather.3
  120.7 21.7 all-gather.5
  176.9 15.7 all-gather.7
  238.7 135.5 all-reduce.37
where the time goes:
time: 392 us; the launch traced here: 385 us
  waiting for transfers between devices  178 us (45%)
  local copies, waits for them, and re-layouts  60 us (15%)
  starting transfers between devices  51.1 us (13%)
  matrix products  39.3 us (10%)
  other arithmetic  27.3 us (7%)
  between operations  17.3 us (4%)
  blocking collectives  12.2 us (3%)
    psum x1, waiting for transfers between devices, body_time(): weight_one, weight_two = lax.psum((sum_one, sum_two), ('tm', 'space'))  134 us
    ppermute x9, starting transfers between devices, padded_2(): lax.ppermute(tail, axis, [(i, (i + 1) % count) for i in range(ends)])  38.1 us
    ppermute x9, waiting for transfers between devices, padded_2(): lax.ppermute(head, axis, [((i + 1) % count, i) for i in range(ends)])  21.9 us
    all_gather x3, waiting for transfers between devices, body_time(): moved = lax.all_gather(to_refs, 'tm', axis=0, tiled=True)  20.7 us
    unnamed x158, local copies, waits for them, and re-layouts  18.8 us
    dot_general x4, matrix products, body_time(): jnp.einsum('kf,kx->fx', weights.astype(jnp.bfloat16), moved.reshape(moved...  14.4 us
    ppermute x9, starting transfers between devices, padded_2(): lax.ppermute(head, axis, [((i + 1) % count, i) for i in range(ends)])  12.7 us
    dot_general x4, matrix products, body_time(): jnp.einsum('sf,fx->sx', picker_wide, act_slope.reshape(frames_dev, -1), p...  9.11 us
  transfers between devices with their start and end apart: 22, of which 13 were waited for; matrix products, arithmetic and copies ran while one was open for 19% of the time, Pallas kernels for 0%

commit v1 on v0

--- a/solution.py
+++ b/solution.py
@@ -3,6 +3,7 @@
 import jax.numpy as jnp
 from jax import lax
 from jax.sharding import PartitionSpec as P
+from jax.lax import axis_index, axis_size, ppermute
 
 
 def padded_2(cells, sides, width):
@@ -146,7 +147,27 @@
         )
         frame_grad = frame_grad.astype(jnp.bfloat16).reshape(kept_grad.shape)
         kept_grad = jnp.where(active[:, None, None], frame_grad, kept_grad)
-        moved = lax.all_gather(to_refs, "tm", axis=0, tiled=True)
+        v1, latest, out_arr = (axis_size("tm"), axis_index("tm"), to_refs.shape[0])
+        moved = lax.dynamic_update_slice_in_dim(
+            jnp.zeros(
+                [to_i * v1 if j0 == 0 else to_i for j0, to_i in enumerate(to_refs.shape)],
+                to_refs.dtype,
+            ),
+            to_refs,
+            latest * out_arr,
+            axis=0,
+        )
+        big = x_next = to_refs
+        for k0 in range(1, v1 // 2 + 1):
+            big = ppermute(big, "tm", perm=[(j0, (j0 + 1) % v1) for j0 in range(v1)])
+            moved = lax.dynamic_update_slice_in_dim(
+                moved, big, (latest - k0) % v1 * out_arr, axis=0
+            )
+            if 2 * k0 < v1:
+                x_next = ppermute(x_next, "tm", perm=[(j0, (j0 - 1) % v1) for j0 in range(v1)])
+                moved = lax.dynamic_update_slice_in_dim(
+                    moved, x_next, (latest + k0) % v1 * out_arr, axis=0
+                )
         sender_ids = lax.all_gather(slot_ids, "tm", axis=0, tiled=True)
         sender_ok = lax.all_gather(slot_ok, "tm", axis=0, tiled=True)
         matches = (sender_ids[:, None] == all_frames[None, :]).astype(jnp.int32)

time: 392 us -> 438 us (1.12)
  starting transfers between devices: 51.1 us -> 70.5 us
  waiting for transfers between devices: 178 us -> 196 us
  other arithmetic: 27.3 us -> 38 us
  local copies, waits for them, and re-layouts: 60 us -> 68 us
  blocking collectives: 12.2 us -> 5.88 us
    ppermute x0 -> x12, waiting for transfers between devices: none -> 56.8 us  [the longest x8 56.4 us: body_time(): big = ppermute(big, 'tm', perm=[(j0, (j0 + 1) % v1) for j0 in range(v1)])]
    ppermute x9, waiting for transfers between devices: 21.9 us -> 0.02 us  [padded_2(): lax.ppermute(head, axis, [((i + 1) % count, i) for i in range(ends)])]
    all_gather x3 -> x0, waiting for transfers between devices: 20.7 us -> none  [body_time(): moved = lax.all_gather(to_refs, 'tm', axis=0, tiled=True)]
    ppermute x9, starting transfers between devices: 38.1 us -> 51.5 us  [padded_2(): lax.ppermute(tail, axis, [(i, (i + 1) % count) for i in range(ends)])]
    ppermute x0 -> x12, starting transfers between devices: none -> 7.17 us  [the longest x4 6.93 us: body_time(): ppermute(x_next, 'tm', perm=[(j0, (j0 - 1) % v1) for j0 in range(v1)])]
    all_gather x1 -> x0, blocking collectives: 6.5 us -> none  [body_time(): moved = lax.all_gather(to_refs, 'tm', axis=0, tiled=True)]
    dot_general x4, matrix products: 14.4 us -> 8.94 us  [body_time(): jnp.einsum('kf,kx->fx', weights.astype(jnp.bfloat16), moved.reshape(moved...]
    unnamed x158 -> x144, local copies, waits for them, and re-layouts: 18.8 us -> 20.6 us
  transfers between devices with their start and end apart: 22 -> 31, of which waited for: 13 -> 13; matrix products, arithmetic and copies ran while one was open for 19% -> 17% of each run, Pallas kernels for 0% -> 0%
where the time goes in v1:
time: 438 us; the launch traced here: 432 us
  waiting for transfers between devices  196 us (45%)
  starting transfers between devices  70.5 us (16%)
  local copies, waits for them, and re-layouts  68 us (16%)
  other arithmetic  38 us (9%)
  matrix products  36.2 us (8%)
  between operations  17.6 us (4%)
  blocking collectives  5.88 us (1%)
    psum x1, waiting for transfers between devices, body_time(): weight_one, weight_two = lax.psum((sum_one, sum_two), ('tm', 'space'))  138 us
    ppermute x8, waiting for transfers between devices, body_time(): big = ppermute(big, 'tm', perm=[(j0, (j0 + 1) % v1) for j0 in range(v1)])  56.4 us
    ppermute x9, starting transfers between devices, padded_2(): lax.ppermute(tail, axis, [(i, (i + 1) % count) for i in range(ends)])  51.5 us
    unnamed x144, local copies, waits for them, and re-layouts  20.6 us
    ppermute x9, starting transfers between devices, padded_2(): lax.ppermute(head, axis, [((i + 1) % count, i) for i in range(ends)])  11.7 us
    dot_general x4, matrix products, body_time(): jnp.einsum('sf,fx->sx', picker_wide, act_slope.reshape(frames_dev, -1), p...  11.3 us
    concatenate x9, other arithmetic, padded_2(): jnp.concatenate([lax.ppermute(tail, axis, [(i, (i + 1) % count) for i in...  9.74 us
    reshape x10, local copies, waits for them, and re-layouts, pair_view(): grid.reshape(field.shape[0], field.shape[1], (col_count + 2) // 2, 2 * ch...  9.61 us
  transfers between devices with their start and end apart: 31, of which 13 were waited for; matrix products, arithmetic and copies ran while one was open for 17% of the time, Pallas kernels for 0%

profile of v1, /device:TPU:0, one launch (start us, length us, event | category | flops | bytes accessed | tf_op | source)
XLA Modules:
  0.0 431.9 jit_solution(9265403373183365008)
XLA Ops:
  14.4 6.2 %collective-permute-start = (bf16[4,1,8192]{2,0,1:T(4,128)(2,1)}, bf16[4,1,8192]{2,0,1:T(4,128)(2,1)}, u32[]{:S(2)}, u32[]{:S(2)}) collective-permute-start(bf16[4,1,8192]{2,0,1:T(4,128)(2,1)} %get-tuple-element.99), channel_id=1, source_target_pairs={{0,1},{1,2},{2,3},{3,4},{4,5},{5,6},{6,7},{8,9},{9,10},{10,11},{11... | collective-permute-start | bytes 196616 | tf_op jit(solution)/shard_map/ppermute | solution.py:17
  24.4 5.6 %collective-permute-start.28 = (bf16[2,4,1,8192]{3,2,1,0:T(2,128)(2,1)}, bf16[2,4,1,8192]{3,2,1,0:T(2,128)(2,1)}, u32[]{:S(2)}, u32[]{:S(2)}) collective-permute-start(bf16[2,4,1,8192]{3,2,1,0:T(2,128)(2,1)} %get-tuple-element.51), channel_id=1, source_target_pairs={{0,1},{1,2},{2,3},{3,4},{4,5},{5,6},{6,7},{8,9},{9,10},{10,11},{11... | collective-permute-start | bytes 393224 | tf_op jit(solution)/shard_map/ppermute | solution.py:17
  37.8 5.9 %all-reduce.34 = (s32[16]{0:T(128)}, s32[16]{0:T(128)}, s32[16]{0:T(128)S(1)}, s32[16]{0:T(128)S(1)}, s32[8]{0:T(128)}, /*index=5*/s32[8]{0:T(128)}, s32[4]{0:T(128)S(1)}, s32[4]{0:T(128)}) all-reduce(s32[16]{0:T(128)S(1)} %dynamic-update-slice.3, s32[16]{0:T(128)S(1)} %dynamic-update-slice.1, ...), channel_id=1, replica_groups=mesh['tm'=4,'space'=8] {'tm'}, use_global_device_ids=true, to_apply=%add.29 | all-reduce | flops 88 | bytes 704
  75.2 4.8 %collective-permute-start.2 = (bf16[4,1,8192]{2,0,1:T(4,128)(2,1)S(1)}, bf16[4,1,8192]{2,0,1:T(4,128)(2,1)S(1)}, u32[]{:S(2)}, u32[]{:S(2)}) collective-permute-start(bf16[4,1,8192]{2,0,1:T(4,128)(2,1)S(1)} %get-tuple-element.97), channel_id=1, source_target_pairs={{0,1},{1,2},{2,3},{3,4},{4,5},{5,6},{6,7},{8,9},{9,10},{10,11},{11... | collective-permute-start | bytes 196616 | tf_op jit(solution)/shard_map/ppermute | solution.py:17
  93.3 9.0 %collective-permute-done.4 = bf16[4,8,8192]{2,1,0:T(8,128)(2,1)S(1)} collective-permute-done((bf16[4,8,8192]{2,1,0:T(8,128)(2,1)S(1)}, bf16[4,8,8192]{2,1,0:T(8,128)(2,1)S(1)}, u32[]{:S(2)}, u32[]{:S(2)}) %collective-permute-start.4) | collective-permute-done | bytes 524320 | tf_op jit(solution)/shard_map/ppermute | solution.py:162
  102.5 8.5 %collective-permute-done.6 = bf16[4,8,8192]{2,1,0:T(8,128)(2,1)S(1)} collective-permute-done((bf16[4,8,8192]{2,1,0:T(8,128)(2,1)S(1)}, bf16[4,8,8192]{2,1,0:T(8,128)(2,1)S(1)}, u32[]{:S(2)}, u32[]{:S(2)}) %collective-permute-start.6) | collective-permute-done | bytes 524320 | tf_op jit(solution)/shard_map/ppermute | solution.py:162
  111.0 4.0 fusion.214
  116.9 5.9 %collective-permute-start.7 = (bf16[4,1,8192]{2,0,1:T(4,128)(2,1)S(1)}, bf16[4,1,8192]{2,0,1:T(4,128)(2,1)S(1)}, u32[]{:S(2)}, u32[]{:S(2)}) collective-permute-start(bf16[4,1,8192]{2,0,1:T(4,128)(2,1)S(1)} %get-tuple-element.95), channel_id=1, source_target_pairs={{0,1},{1,2},{2,3},{3,4},{4,5},{5,6},{6,7},{8,9},{9,10},{10,11},{11... | collective-permute-start | bytes 196616 | tf_op jit(solution)/shard_map/ppermute | solution.py:17
  138.2 3.6 fusion.1
  144.0 6.0 %collective-permute-start.9 = (bf16[4,1,8192]{2,0,1:T(4,128)(2,1)S(1)}, bf16[4,1,8192]{2,0,1:T(4,128)(2,1)S(1)}, u32[]{:S(2)}, u32[]{:S(2)}) collective-permute-start(bf16[4,1,8192]{2,0,1:T(4,128)(2,1)S(1)} %get-tuple-element.93), channel_id=1, source_target_pairs={{0,1},{1,2},{2,3},{3,4},{4,5},{5,6},{6,7},{8,9},{9,10},{10,11},{11... | collective-permute-start | bytes 196616 | tf_op jit(solution)/shard_map/ppermute | solution.py:17
  169.0 11.3 %collective-permute-done.11 = bf16[4,8,8192]{2,1,0:T(8,128)(2,1)S(1)} collective-permute-done((bf16[4,8,8192]{2,1,0:T(8,128)(2,1)S(1)}, bf16[4,8,8192]{2,1,0:T(8,128)(2,1)S(1)}, u32[]{:S(2)}, u32[]{:S(2)}) %collective-permute-start.11) | collective-permute-done | bytes 524320 | tf_op jit(solution)/shard_map/ppermute | solution.py:162
  180.4 8.5 %collective-permute-done.13 = bf16[4,8,8192]{2,1,0:T(8,128)(2,1)S(1)} collective-permute-done((bf16[4,8,8192]{2,1,0:T(8,128)(2,1)S(1)}, bf16[4,8,8192]{2,1,0:T(8,128)(2,1)S(1)}, u32[]{:S(2)}, u32[]{:S(2)}) %collective-permute-start.13) | collective-permute-done | bytes 524320 | tf_op jit(solution)/shard_map/ppermute | solution.py:162
  189.0 2.5 fusion.215
  193.3 5.6 %collective-permute-start.14 = (bf16[2,1,8192]{2,0,1:T(2,128)(2,1)S(1)}, bf16[2,1,8192]{2,0,1:T(2,128)(2,1)S(1)}, u32[]{:S(2)}, u32[]{:S(2)}) collective-permute-start(bf16[2,1,8192]{2,0,1:T(2,128)(2,1)S(1)} %get-tuple-element.107), channel_id=1, source_target_pairs={{0,1},{1,2},{2,3},{3,4},{4,5},{5,6},{6,7},{8,9},{9,10},{10,11},{11... | collective-permute-start | bytes 98312 | tf_op jit(solution)/shard_map/ppermute | solution.py:17
  205.5 3.0 fusion.2
  209.8 5.4 %collective-permute-start.16 = (bf16[2,1,8192]{2,0,1:T(2,128)(2,1)S(1)}, bf16[2,1,8192]{2,0,1:T(2,128)(2,1)S(1)}, u32[]{:S(2)}, u32[]{:S(2)}) collective-permute-start(bf16[2,1,8192]{2,0,1:T(2,128)(2,1)S(1)} %get-tuple-element.105), channel_id=1, source_target_pairs={{0,1},{1,2},{2,3},{3,4},{4,5},{5,6},{6,7},{8,9},{9,10},{10,11},{11... | collective-permute-start | bytes 98312 | tf_op jit(solution)/shard_map/ppermute | solution.py:17
  221.9 6.7 %collective-permute-done.18 = bf16[2,8,8192]{2,1,0:T(8,128)(2,1)S(1)} collective-permute-done((bf16[2,8,8192]{2,1,0:T(8,128)(2,1)S(1)}, bf16[2,8,8192]{2,1,0:T(8,128)(2,1)S(1)}, u32[]{:S(2)}, u32[]{:S(2)}) %collective-permute-start.18) | collective-permute-done | bytes 262176 | tf_op jit(solution)/shard_map/ppermute | solution.py:162
  228.7 5.7 %collective-permute-done.20 = bf16[2,8,8192]{2,1,0:T(8,128)(2,1)S(1)} collective-permute-done((bf16[2,8,8192]{2,1,0:T(8,128)(2,1)S(1)}, bf16[2,8,8192]{2,1,0:T(8,128)(2,1)S(1)}, u32[]{:S(2)}, u32[]{:S(2)}) %collective-permute-start.20) | collective-permute-done | bytes 262176 | tf_op jit(solution)/shard_map/ppermute | solution.py:162
  237.8 5.7 %collective-permute-start.21 = (bf16[1,1,8192]{2,1,0:T(2,128)(2,1)S(1)}, bf16[1,1,8192]{2,1,0:T(2,128)(2,1)S(1)}, u32[]{:S(2)}, u32[]{:S(2)}) collective-permute-start(bf16[1,1,8192]{2,1,0:T(2,128)(2,1)S(1)} %get-tuple-element.139), channel_id=1, source_target_pairs={{0,1},{1,2},{2,3},{3,4},{4,5},{5,6},{6,7},{8,9},{9,10},{10,11},{11... | collective-permute-start | bytes 49160 | tf_op jit(solution)/shard_map/ppermute | solution.py:17
  252.1 6.4 %collective-permute-start.23 = (bf16[1,1,8192]{2,1,0:T(2,128)(2,1)}, bf16[1,1,8192]{2,1,0:T(2,128)(2,1)}, u32[]{:S(2)}, u32[]{:S(2)}) collective-permute-start(bf16[1,1,8192]{2,1,0:T(2,128)(2,1)} %get-tuple-element.137), channel_id=1, source_target_pairs={{0,1},{1,2},{2,3},{3,4},{4,5},{5,6},{6,7},{8,9},{9,10},{10,11},{11... | collective-permute-start | bytes 49160 | tf_op jit(solution)/shard_map/ppermute | solution.py:17
  265.1 2.6 collective-permute-done.25
  268.1 4.0 collective-permute-done.27
  283.2 137.9 %all-reduce.38.cloned.1.call-done = (f32[4,3,3,64,64]{4,3,2,1,0:T(8,128)}, f32[4,3,3,64,64]{4,3,2,1,0:T(8,128)}) async-done(((f32[4,3,3,64,64]{4,3,2,1,0:T(8,128)}, f32[4,3,3,64,64]{4,3,2,1,0:T(8,128)}), (f32[4,3,3,64,64]{4,3,2,1,0:T(8,128)}, f32[4,3,3,64,64]{4,3,2,1,0:T(8,128)})) %all-reduce.38.cloned.1.call-update) | async-done | bytes 1179664 | tf_op jit(solution)/shard_map/psum | solution.py:196
  421.1 2.5 copy.332
  (397 shorter events, 147.1 us)
Async XLA Ops:
  7.2 413.9 %all-reduce.38.cloned.1.call-start = ((), (), s32[]{:S(2)}) async-start(), calls=%async_computation | async-start | bytes 4718592 | tf_op jit(solution)/shard_map/psum | solution.py:196
  13.1 50.3 %collective-permute-start.1 = (bf16[4,1,8192]{2,0,1:T(4,128)(2,1)}, bf16[4,1,8192]{2,0,1:T(4,128)(2,1)}, u32[]{:S(2)}, u32[]{:S(2)}) collective-permute-start(bf16[4,1,8192]{2,0,1:T(4,128)(2,1)} %get-tuple-element.100), channel_id=1, source_target_pairs={{1,0},{2,1},{3,2},{4,3},{5,4},{6,5},{7,6},{9,8},{10,9},{11,10},{12... | collective-permute-start | bytes 196616 | tf_op jit(solution)/shard_map/ppermute | solution.py:19
  14.4 50.6 %collective-permute-start = (bf16[4,1,8192]{2,0,1:T(4,128)(2,1)}, bf16[4,1,8192]{2,0,1:T(4,128)(2,1)}, u32[]{:S(2)}, u32[]{:S(2)}) collective-permute-start(bf16[4,1,8192]{2,0,1:T(4,128)(2,1)} %get-tuple-element.99), channel_id=1, source_target_pairs={{0,1},{1,2},{2,3},{3,4},{4,5},{5,6},{6,7},{8,9},{9,10},{10,11},{11... | collective-permute-start | bytes 196616 | tf_op jit(solution)/shard_map/ppermute | solution.py:17
  23.1 68.0 %collective-permute-start.29 = (bf16[2,4,1,8192]{3,2,1,0:T(2,128)(2,1)}, bf16[2,4,1,8192]{3,2,1,0:T(2,128)(2,1)}, u32[]{:S(2)}, u32[]{:S(2)}) collective-permute-start(bf16[2,4,1,8192]{3,2,1,0:T(2,128)(2,1)} %get-tuple-element.52), channel_id=1, source_target_pairs={{1,0},{2,1},{3,2},{4,3},{5,4},{6,5},{7,6},{9,8},{10,9},{11,10},{12... | collective-permute-start | bytes 393224 | tf_op jit(solution)/shard_map/ppermute | solution.py:19
  24.4 66.7 %collective-permute-start.28 = (bf16[2,4,1,8192]{3,2,1,0:T(2,128)(2,1)}, bf16[2,4,1,8192]{3,2,1,0:T(2,128)(2,1)}, u32[]{:S(2)}, u32[]{:S(2)}) collective-permute-start(bf16[2,4,1,8192]{3,2,1,0:T(2,128)(2,1)} %get-tuple-element.51), channel_id=1, source_target_pairs={{0,1},{1,2},{2,3},{3,4},{4,5},{5,6},{6,7},{8,9},{9,10},{10,11},{11... | collective-permute-start | bytes 393224 | tf_op jit(solution)/shard_map/ppermute | solution.py:17
  73.9 7.4 %collective-permute-start.3 = (bf16[4,1,8192]{2,0,1:T(4,128)(2,1)S(1)}, bf16[4,1,8192]{2,0,1:T(4,128)(2,1)S(1)}, u32[]{:S(2)}, u32[]{:S(2)}) collective-permute-start(bf16[4,1,8192]{2,0,1:T(4,128)(2,1)S(1)} %get-tuple-element.98), channel_id=1, source_target_pairs={{1,0},{2,1},{3,2},{4,3},{5,4},{6,5},{7,6},{9,8},{10,9},{11,10},{12... | collective-permute-start | bytes 196616 | tf_op jit(solution)/shard_map/ppermute | solution.py:19
  89.2 13.1 %collective-permute-start.4 = (bf16[4,8,8192]{2,1,0:T(8,128)(2,1)S(1)}, bf16[4,8,8192]{2,1,0:T(8,128)(2,1)S(1)}, u32[]{:S(2)}, u32[]{:S(2)}) collective-permute-start(bf16[4,8,8192]{2,1,0:T(8,128)(2,1)S(1)} %convert_element_type.213), channel_id=1, source_target_pairs={{0,8},{8,16},{16,24},{24,0},{1,9},{9,17},{17,25},{25,1},{2,10},{10... | collective-permute-start | bytes 1572872 | tf_op jit(solution)/shard_map/ppermute | solution.py:162
  89.3 13.1 %collective-permute-start.5 = (bf16[4,8,8192]{2,1,0:T(8,128)(2,1)S(1)}, bf16[4,8,8192]{2,1,0:T(8,128)(2,1)S(1)}, u32[]{:S(2)}, u32[]{:S(2)}) collective-permute-start(bf16[4,8,8192]{2,1,0:T(8,128)(2,1)S(1)} %convert_element_type.213), channel_id=1, source_target_pairs={{0,24},{8,0},{16,8},{24,16},{1,25},{9,1},{17,9},{25,17},{2,26},{10... | collective-permute-start | bytes 1572872 | tf_op jit(solution)/shard_map/ppermute | solution.py:167
  102.4 8.6 %collective-permute-start.6 = (bf16[4,8,8192]{2,1,0:T(8,128)(2,1)S(1)}, bf16[4,8,8192]{2,1,0:T(8,128)(2,1)S(1)}, u32[]{:S(2)}, u32[]{:S(2)}) collective-permute-start(bf16[4,8,8192]{2,1,0:T(8,128)(2,1)S(1)} %collective-permute-done.4), channel_id=1, source_target_pairs={{0,8},{8,16},{16,24},{24,0},{1,9},{9,17},{17,25},{25,1},{2,10},{10... | collective-permute-start | bytes 1572872 | tf_op jit(solution)/shard_map/ppermute | solution.py:162
  115.6 15.3 %collective-permute-start.8 = (bf16[4,1,8192]{2,0,1:T(4,128)(2,1)S(1)}, bf16[4,1,8192]{2,0,1:T(4,128)(2,1)S(1)}, u32[]{:S(2)}, u32[]{:S(2)}) collective-permute-start(bf16[4,1,8192]{2,0,1:T(4,128)(2,1)S(1)} %get-tuple-element.96), channel_id=1, source_target_pairs={{1,0},{2,1},{3,2},{4,3},{5,4},{6,5},{7,6},{9,8},{10,9},{11,10},{12... | collective-permute-start | bytes 196616 | tf_op jit(solution)/shard_map/ppermute | solution.py:19
  116.9 14.2 %collective-permute-start.7 = (bf16[4,1,8192]{2,0,1:T(4,128)(2,1)S(1)}, bf16[4,1,8192]{2,0,1:T(4,128)(2,1)S(1)}, u32[]{:S(2)}, u32[]{:S(2)}) collective-permute-start(bf16[4,1,8192]{2,0,1:T(4,128)(2,1)S(1)} %get-tuple-element.95), channel_id=1, source_target_pairs={{0,1},{1,2},{2,3},{3,4},{4,5},{5,6},{6,7},{8,9},{9,10},{10,11},{11... | collective-permute-start | bytes 196616 | tf_op jit(solution)/shard_map/ppermute | solution.py:17
  142.6 13.8 %collective-permute-start.10 = (bf16[4,1,8192]{2,0,1:T(4,128)(2,1)S(1)}, bf16[4,1,8192]{2,0,1:T(4,128)(2,1)S(1)}, u32[]{:S(2)}, u32[]{:S(2)}) collective-permute-start(bf16[4,1,8192]{2,0,1:T(4,128)(2,1)S(1)} %get-tuple-element.94), channel_id=1, source_target_pairs={{1,0},{2,1},{3,2},{4,3},{5,4},{6,5},{7,6},{9,8},{10,9},{11,10},{12... | collective-permute-start | bytes 196616 | tf_op jit(solution)/shard_map/ppermute | solution.py:19
  144.0 12.4 %collective-permute-start.9 = (bf16[4,1,8192]{2,0,1:T(4,128)(2,1)S(1)}, bf16[4,1,8192]{2,0,1:T(4,128)(2,1)S(1)}, u32[]{:S(2)}, u32[]{:S(2)}) collective-permute-start(bf16[4,1,8192]{2,0,1:T(4,128)(2,1)S(1)} %get-tuple-element.93), channel_id=1, source_target_pairs={{0,1},{1,2},{2,3},{3,4},{4,5},{5,6},{6,7},{8,9},{9,10},{10,11},{11... | collective-permute-start | bytes 196616 | tf_op jit(solution)/shard_map/ppermute | solution.py:17
  166.9 13.4 %collective-permute-start.11 = (bf16[4,8,8192]{2,1,0:T(8,128)(2,1)S(1)}, bf16[4,8,8192]{2,1,0:T(8,128)(2,1)S(1)}, u32[]{:S(2)}, u32[]{:S(2)}) collective-permute-start(bf16[4,8,8192]{2,1,0:T(8,128)(2,1)S(1)} %convert_element_type.223), channel_id=1, source_target_pairs={{0,8},{8,16},{16,24},{24,0},{1,9},{9,17},{17,25},{25,1},{2,10},{10... | collective-permute-start | bytes 1572872 | tf_op jit(solution)/shard_map/ppermute | solution.py:162
  166.9 13.4 %collective-permute-start.12 = (bf16[4,8,8192]{2,1,0:T(8,128)(2,1)S(1)}, bf16[4,8,8192]{2,1,0:T(8,128)(2,1)S(1)}, u32[]{:S(2)}, u32[]{:S(2)}) collective-permute-start(bf16[4,8,8192]{2,1,0:T(8,128)(2,1)S(1)} %convert_element_type.223), channel_id=1, source_target_pairs={{0,24},{8,0},{16,8},{24,16},{1,25},{9,1},{17,9},{25,17},{2,26},{10... | collective-permute-start | bytes 1572872 | tf_op jit(solution)/shard_map/ppermute | solution.py:167
  180.3 8.6 %collective-permute-start.13 = (bf16[4,8,8192]{2,1,0:T(8,128)(2,1)S(1)}, bf16[4,8,8192]{2,1,0:T(8,128)(2,1)S(1)}, u32[]{:S(2)}, u32[]{:S(2)}) collective-permute-start(bf16[4,8,8192]{2,1,0:T(8,128)(2,1)S(1)} %collective-permute-done.11), channel_id=1, source_target_pairs={{0,8},{8,16},{16,24},{24,0},{1,9},{9,17},{17,25},{25,1},{2,10},{10... | collective-permute-start | bytes 1572872 | tf_op jit(solution)/shard_map/ppermute | solution.py:162
  192.0 8.6 %collective-permute-start.15 = (bf16[2,1,8192]{2,0,1:T(2,128)(2,1)S(1)}, bf16[2,1,8192]{2,0,1:T(2,128)(2,1)S(1)}, u32[]{:S(2)}, u32[]{:S(2)}) collective-permute-start(bf16[2,1,8192]{2,0,1:T(2,128)(2,1)S(1)} %get-tuple-element.108), channel_id=1, source_target_pairs={{1,0},{2,1},{3,2},{4,3},{5,4},{6,5},{7,6},{9,8},{10,9},{11,10},{12... | collective-permute-start | bytes 98312 | tf_op jit(solution)/shard_map/ppermute | solution.py:19
  193.3 7.4 %collective-permute-start.14 = (bf16[2,1,8192]{2,0,1:T(2,128)(2,1)S(1)}, bf16[2,1,8192]{2,0,1:T(2,128)(2,1)S(1)}, u32[]{:S(2)}, u32[]{:S(2)}) collective-permute-start(bf16[2,1,8192]{2,0,1:T(2,128)(2,1)S(1)} %get-tuple-element.107), channel_id=1, source_target_pairs={{0,1},{1,2},{2,3},{3,4},{4,5},{5,6},{6,7},{8,9},{9,10},{10,11},{11... | collective-permute-start | bytes 98312 | tf_op jit(solution)/shard_map/ppermute | solution.py:17
  208.5 8.0 %collective-permute-start.17 = (bf16[2,1,8192]{2,0,1:T(2,128)(2,1)S(1)}, bf16[2,1,8192]{2,0,1:T(2,128)(2,1)S(1)}, u32[]{:S(2)}, u32[]{:S(2)}) collective-permute-start(bf16[2,1,8192]{2,0,1:T(2,128)(2,1)S(1)} %get-tuple-element.106), channel_id=1, source_target_pairs={{1,0},{2,1},{3,2},{4,3},{5,4},{6,5},{7,6},{9,8},{10,9},{11,10},{12... | collective-permute-start | bytes 98312 | tf_op jit(solution)/shard_map/ppermute | solution.py:19
  220.0 8.6 %collective-permute-start.18 = (bf16[2,8,8192]{2,1,0:T(8,128)(2,1)S(1)}, bf16[2,8,8192]{2,1,0:T(8,128)(2,1)S(1)}, u32[]{:S(2)}, u32[]{:S(2)}) collective-permute-start(bf16[2,8,8192]{2,1,0:T(8,128)(2,1)S(1)} %convert_element_type.233), channel_id=1, source_target_pairs={{0,8},{8,16},{16,24},{24,0},{1,9},{9,17},{17,25},{25,1},{2,10},{10... | collective-permute-start | bytes 786440 | tf_op jit(solution)/shard_map/ppermute | solution.py:162
  220.1 8.6 %collective-permute-start.19 = (bf16[2,8,8192]{2,1,0:T(8,128)(2,1)S(1)}, bf16[2,8,8192]{2,1,0:T(8,128)(2,1)S(1)}, u32[]{:S(2)}, u32[]{:S(2)}) collective-permute-start(bf16[2,8,8192]{2,1,0:T(8,128)(2,1)S(1)} %convert_element_type.233), channel_id=1, source_target_pairs={{0,24},{8,0},{16,8},{24,16},{1,25},{9,1},{17,9},{25,17},{2,26},{10... | collective-permute-start | bytes 786440 | tf_op jit(solution)/shard_map/ppermute | solution.py:167
  236.5 7.7 %collective-permute-start.22 = (bf16[1,1,8192]{2,1,0:T(2,128)(2,1)S(1)}, bf16[1,1,8192]{2,1,0:T(2,128)(2,1)S(1)}, u32[]{:S(2)}, u32[]{:S(2)}) collective-permute-start(bf16[1,1,8192]{2,1,0:T(2,128)(2,1)S(1)} %get-tuple-element.140), channel_id=1, source_target_pairs={{1,0},{2,1},{3,2},{4,3},{5,4},{6,5},{7,6},{9,8},{10,9},{11,10},{12... | collective-permute-start | bytes 49160 | tf_op jit(solution)/shard_map/ppermute | solution.py:19
  250.8 9.3 %collective-permute-start.24 = (bf16[1,1,8192]{2,1,0:T(2,128)(2,1)}, bf16[1,1,8192]{2,1,0:T(2,128)(2,1)}, u32[]{:S(2)}, u32[]{:S(2)}) collective-permute-start(bf16[1,1,8192]{2,1,0:T(2,128)(2,1)} %get-tuple-element.138), channel_id=1, source_target_pairs={{1,0},{2,1},{3,2},{4,3},{5,4},{6,5},{7,6},{9,8},{10,9},{11,10},{12... | collective-permute-start | bytes 49160 | tf_op jit(solution)/shard_map/ppermute | solution.py:19
  252.1 8.9 %collective-permute-start.23 = (bf16[1,1,8192]{2,1,0:T(2,128)(2,1)}, bf16[1,1,8192]{2,1,0:T(2,128)(2,1)}, u32[]{:S(2)}, u32[]{:S(2)}) collective-permute-start(bf16[1,1,8192]{2,1,0:T(2,128)(2,1)} %get-tuple-element.137), channel_id=1, source_target_pairs={{0,1},{1,2},{2,3},{3,4},{4,5},{5,6},{6,7},{8,9},{9,10},{10,11},{11... | collective-permute-start | bytes 49160 | tf_op jit(solution)/shard_map/ppermute | solution.py:17
  (62 other events, 483.1 us)
Sparse Core Ops, SparseCore 0:
  281.7 139.2 all-reduce.37
